TPU v7x, 512 devices: a whole 4x8x8 slice. The times are simulated.
512 devices in a mesh: elem: 32 (over y_lo, z), orb: 16 (over x, y_hi, core).
Axes of the slice: x: 4, y: 8 (y_hi: 2, y_lo: 4; y = y_hi * 4 + y_lo), z: 8, core: 2. Of those that a mesh axis runs over, the one named last changes fastest.
Arguments:
- orbitals: bfloat16 [24576, 4096], P('elem', 'orb')
- hamiltonian: bfloat16 [384, 7, 64, 64], P('elem'), may hold values from -0.25 to 0.25
- neighbours: int32 [384, 7], P('elem'), may hold values from 0 to 383, as said below
Outputs:
- updated: bfloat16 [24576, 4096], P('elem', 'orb')
Inputs may be any that keep to these rules, and one draw needn't show every extreme that they name: Elements form tiles of 12 consecutive indices, each tile a periodic 3 x 4 plane of elements in some order, tiles stacked periodically. An element's row lists itself, its two neighbours along each in-plane direction, then the element at the same place in the previous tile and in the next tile.
All inputs are finite; a program needn't handle non-finite values.
Results may differ from a plain program's by a relative error of at most 0.0062.
Values may be sent and summed in bfloat16 or wider, within the bound.
A program may use at most 64 MiB of HBM per device.

v0:
```python
import jax
import jax.numpy as jnp
from jax import lax
from jax.sharding import PartitionSpec as P


def extended_2(value, sides, width):
    for axis, dim in sides:
        peers, length = (lax.axis_size(axis), value.shape[dim])
        up = [(i, (i + 1) % peers) for i in range(peers)]
        down = [(j, i) for i, j in up]
        last = lax.slice_in_dim(value, length - width, length, axis=dim)
        initial = lax.slice_in_dim(value, 0, width, axis=dim)
        before = lax.ppermute(last, axis, up)
        after = lax.ppermute(initial, axis, down)
        value = jnp.concatenate([before, value, after], axis=dim)
    return value


def neighbour_product(hamiltonian, local_index, field):
    rows, width = field.shape
    elements = hamiltonian.shape[0]
    block_size = hamiltonian.shape[2]
    extended = extended_2(field, (("elem", 0),), rows)
    blocks = extended.reshape(3 * elements, block_size, width)
    picked = blocks[local_index]
    result = jnp.einsum("enab,enbc->eac", hamiltonian, picked, preferred_element_type=jnp.float32)
    return result.reshape(rows, width)


def local(orbitals, hamiltonian, neighbours):
    elements = hamiltonian.shape[0]
    tiles = lax.axis_size("elem")
    my_tile = lax.axis_index("elem")
    other_tile = neighbours // elements
    relative = (other_tile - my_tile + tiles) % tiles
    slot = jnp.where(relative == 0, 1, jnp.where(relative == 1, 2, 0)).astype(jnp.int32)
    local_index = slot * elements + neighbours % elements
    start_field = orbitals.astype(jnp.float32)
    first = neighbour_product(hamiltonian, local_index, orbitals)
    first_half = first.astype(jnp.bfloat16)
    second = 2.0 * neighbour_product(hamiltonian, local_index, first_half) - start_field
    second_half = second.astype(jnp.bfloat16)
    third = 2.0 * neighbour_product(hamiltonian, local_index, second_half) - first
    filtered = third.astype(jnp.bfloat16)
    rows_total = filtered.shape[0] * tiles
    columns = filtered.shape[1]
    groups = lax.axis_size("orb")
    my_group = lax.axis_index("orb")
    orbital_count = columns * groups
    panel = lax.all_gather(filtered, "orb", axis=1, tiled=True)
    partial_gram = lax.dot_general(
        panel, filtered, (((0,), (0,)), ((), ())), preferred_element_type=jnp.float32
    )
    gram_part = lax.psum_scatter(partial_gram, "elem", scatter_dimension=0, tiled=True)
    share = gram_part.shape[0]
    row_global = my_tile * share + lax.broadcasted_iota(jnp.int32, gram_part.shape, 0)
    col_global = my_group * columns + lax.broadcasted_iota(jnp.int32, gram_part.shape, 1)
    own_diagonal = jnp.sum(jnp.where(row_global == col_global, gram_part, 0.0))
    total = lax.psum(own_diagonal, ("elem", "orb"))
    level = total / (orbital_count * rows_total)
    scaled_part = (gram_part / (level * rows_total)).astype(jnp.bfloat16)
    scaled = lax.all_gather(scaled_part, "elem", axis=0, tiled=True)
    mixed = jnp.dot(panel, scaled, preferred_element_type=jnp.float32)
    result = (1.5 * filtered.astype(jnp.float32) - 0.5 * mixed) / jnp.sqrt(level)
    return result.astype(jnp.bfloat16)


def solution(mesh):
    return jax.shard_map(
        local,
        mesh=mesh,
        in_specs=(P("elem", "orb"), P("elem", None, None, None), P("elem", None)),
        out_specs=P("elem", "orb"),
        check_vma=False,
    )
```

profile of v0, /device:TPU:2, one launch (start us, length us, event | category | flops | bytes accessed | tf_op | source)
XLA Modules:
  0.0 612.7 jit_solution(15075717939295863914)
XLA Ops:
  6.5 0.0 copy-start
  6.5 0.0 all-gather.3.cloned.1.call-start
  6.5 4.4 collective-permute-start
  10.9 11.6 %collective-permute-start.1 = (bf16[768,256]{1,0:T(8,128)(2,1)}, bf16[768,256]{1,0:T(8,128)(2,1)S(1)}, u32[]{:S(2)}, u32[]{:S(2)}) collective-permute-start(bf16[768,256]{1,0:T(8,128)(2,1)} %param.3), channel_id=1, source_target_pairs={{16,0},{32,16},{48,32},{64,48},{80,64},{96,80},{112,96},{128,112},... | collective-permute-start | bytes 1179656 | tf_op jit(solution)/shard_map/ppermute | solution.py:15
  22.6 0.7 compare_select_fusion
  23.3 0.1 copy.5
  23.4 0.1 reshape.24
  23.5 6.5 %collective-permute-done = bf16[768,256]{1,0:T(8,128)(2,1)S(1)} collective-permute-done((bf16[768,256]{1,0:T(8,128)(2,1)}, bf16[768,256]{1,0:T(8,128)(2,1)S(1)}, u32[]{:S(2)}, u32[]{:S(2)}) %collective-permute-start) | collective-permute-done | bytes 393248 | tf_op jit(solution)/shard_map/ppermute | solution.py:14
  30.0 1.3 collective-permute-done.1
  31.3 1.1 pad_maximum_fusion
  32.3 2.4 gather_fusion
  34.8 0.0 copy-done
  34.8 2.4 fusion.13
  37.2 1.9 collective-permute-start.2
  39.1 8.2 %collective-permute-start.3 = (bf16[768,256]{1,0:T(8,128)(2,1)S(1)}, bf16[768,256]{1,0:T(8,128)(2,1)S(1)}, u32[]{:S(2)}, u32[]{:S(2)}) collective-permute-start(bf16[768,256]{1,0:T(8,128)(2,1)S(1)} %bitcast.52), channel_id=1, source_target_pairs={{16,0},{32,16},{48,32},{64,48},{80,64},{96,80},{112,96},{128,112},... | collective-permute-start | bytes 1179656 | tf_op jit(solution)/shard_map/ppermute | solution.py:15
  47.3 6.3 %collective-permute-done.2 = bf16[768,256]{1,0:T(8,128)(2,1)S(1)} collective-permute-done((bf16[768,256]{1,0:T(8,128)(2,1)S(1)}, bf16[768,256]{1,0:T(8,128)(2,1)S(1)}, u32[]{:S(2)}, u32[]{:S(2)}) %collective-permute-start.2) | collective-permute-done | bytes 393248 | tf_op jit(solution)/shard_map/ppermute | solution.py:14
  53.6 1.2 collective-permute-done.3
  54.8 0.1 pad_maximum_fusion.1
  54.9 2.4 gather_fusion.1
  57.3 0.0 copy-start.1
  57.3 2.4 fusion.2
  59.8 0.0 copy-done.1
  59.8 0.1 fusion.7
  59.9 1.9 collective-permute-start.4
  61.8 8.3 %collective-permute-start.5 = (bf16[768,256]{1,0:T(8,128)(2,1)S(1)}, bf16[768,256]{1,0:T(8,128)(2,1)S(1)}, u32[]{:S(2)}, u32[]{:S(2)}) collective-permute-start(bf16[768,256]{1,0:T(8,128)(2,1)S(1)} %fusion.7), channel_id=1, source_target_pairs={{16,0},{32,16},{48,32},{64,48},{80,64},{96,80},{112,96},{128,112},... | collective-permute-start | bytes 1179656 | tf_op jit(solution)/shard_map/ppermute | solution.py:15
  70.1 5.5 collective-permute-done.4
  75.6 1.2 collective-permute-done.5
  76.7 0.1 pad_maximum_fusion.2
  76.8 2.4 gather_fusion.2
  79.3 3.1 fusion.4
  82.4 0.0 all-gather.3.cloned.1.call-update
  82.4 0.0 reduce-scatter.2.cloned.1.call-start
  82.5 91.5 %all-gather.3.cloned.1.call-done = bf16[768,4096]{1,0:T(8,128)(2,1)} async-done(((bf16[768,256]{1,0:T(8,128)(2,1)}), bf16[768,4096]{1,0:T(8,128)(2,1)}) %all-gather.3.cloned.1.call-update) | async-done | bytes 6291472 | tf_op jit(solution)/shard_map/all_gather | solution.py:51
  174.0 6.7 %fusion.14 = f32[4096,256]{1,0:T(8,128)} fusion(bf16[768,4096]{1,0:T(8,128)(2,1)} %all-gather.3.cloned.1.call-done, bf16[768,256]{1,0:T(8,128)(2,1)} %bitcast.55), kind=kOutput, calls=%fused_computation.37 | convolution fusion | flops 1610612736 | bytes 10878976 | tf_op jit(solution)/shard_map/dot_general | solution.py:52
  180.7 0.0 copy-start.2
  180.7 0.0 reduce-scatter.2.cloned.1.call-update
  180.7 0.0 all-gather.5.cloned.1.call-start
  180.8 172.7 %reduce-scatter.2.cloned.1.call-done = f32[128,256]{1,0:T(8,128)} async-done(((f32[4096,256]{1,0:T(8,128)}), f32[128,256]{1,0:T(8,128)}) %reduce-scatter.2.cloned.1.call-update) | async-done | bytes 131088 | tf_op jit(solution)/shard_map/reduce_scatter | solution.py:55
  353.5 1.6 select_reduce_fusion
  355.1 93.4 %psum.7 = f32[]{:T(128)} all-reduce(f32[]{:T(128)} %select_reduce_fusion), channel_id=1, replica_groups=mesh['elem'=32,'orb'=16] {'elem','orb'}, use_global_device_ids=true, to_apply=%region_2.3 | all-reduce | flops 1 | bytes 8 | tf_op jit(solution)/shard_map/psum | solution.py:60
  449.1 1.5 divide_convert_fusion
  450.6 0.0 all-gather.5.cloned.1.call-update
  451.2 149.0 %all-gather.5.cloned.1.call-done = bf16[4096,256]{1,0:T(8,128)(2,1)} async-done(((bf16[128,256]{1,0:T(8,128)(2,1)}), bf16[4096,256]{1,0:T(8,128)(2,1)}) %all-gather.5.cloned.1.call-update) | async-done | bytes 2097168 | tf_op jit(solution)/shard_map/all_gather | solution.py:63
  600.3 0.0 copy-done.2
  600.3 6.0 fusion.6
  (3 shorter events, 0.0 us)
Async XLA Ops:
  6.5 28.2 %copy-start = (bf16[12,7,64,64]{3,2,1,0:T(8,128)(2,1)S(1)}, bf16[12,7,64,64]{3,2,1,0:T(8,128)(2,1)}, u32[]{:S(2)}) copy-start(bf16[12,7,64,64]{3,2,1,0:T(8,128)(2,1)} %param.4) | copy-start | bytes 2064388
  6.5 167.4 %all-gather.3.cloned.1.call-start = ((), (), s32[]{:S(2)}) async-start(), calls=%async_computation.1 | async-start | bytes 6684672 | tf_op jit(solution)/shard_map/all_gather | solution.py:51
  6.5 23.4 %collective-permute-start = (bf16[768,256]{1,0:T(8,128)(2,1)}, bf16[768,256]{1,0:T(8,128)(2,1)S(1)}, u32[]{:S(2)}, u32[]{:S(2)}) collective-permute-start(bf16[768,256]{1,0:T(8,128)(2,1)} %param.3), channel_id=1, source_target_pairs={{0,16},{16,32},{32,48},{48,64},{64,80},{80,96},{96,112},{112,128},... | collective-permute-start | bytes 1179656 | tf_op jit(solution)/shard_map/ppermute | solution.py:14
  10.9 20.3 %collective-permute-start.1 = (bf16[768,256]{1,0:T(8,128)(2,1)}, bf16[768,256]{1,0:T(8,128)(2,1)S(1)}, u32[]{:S(2)}, u32[]{:S(2)}) collective-permute-start(bf16[768,256]{1,0:T(8,128)(2,1)} %param.3), channel_id=1, source_target_pairs={{16,0},{32,16},{48,32},{64,48},{80,64},{96,80},{112,96},{128,112},... | collective-permute-start | bytes 1179656 | tf_op jit(solution)/shard_map/ppermute | solution.py:15
  37.2 16.4 %collective-permute-start.2 = (bf16[768,256]{1,0:T(8,128)(2,1)S(1)}, bf16[768,256]{1,0:T(8,128)(2,1)S(1)}, u32[]{:S(2)}, u32[]{:S(2)}) collective-permute-start(bf16[768,256]{1,0:T(8,128)(2,1)S(1)} %bitcast.51), channel_id=1, source_target_pairs={{0,16},{16,32},{32,48},{48,64},{64,80},{80,96},{96,112},{112,128},... | collective-permute-start | bytes 1179656 | tf_op jit(solution)/shard_map/ppermute | solution.py:14
  39.1 15.7 %collective-permute-start.3 = (bf16[768,256]{1,0:T(8,128)(2,1)S(1)}, bf16[768,256]{1,0:T(8,128)(2,1)S(1)}, u32[]{:S(2)}, u32[]{:S(2)}) collective-permute-start(bf16[768,256]{1,0:T(8,128)(2,1)S(1)} %bitcast.52), channel_id=1, source_target_pairs={{16,0},{32,16},{48,32},{64,48},{80,64},{96,80},{112,96},{128,112},... | collective-permute-start | bytes 1179656 | tf_op jit(solution)/shard_map/ppermute | solution.py:15
  57.3 2.4 copy-start.1
  59.9 15.7 %collective-permute-start.4 = (bf16[768,256]{1,0:T(8,128)(2,1)S(1)}, bf16[768,256]{1,0:T(8,128)(2,1)S(1)}, u32[]{:S(2)}, u32[]{:S(2)}) collective-permute-start(bf16[768,256]{1,0:T(8,128)(2,1)S(1)} %fusion.7), channel_id=1, source_target_pairs={{0,16},{16,32},{32,48},{48,64},{64,80},{80,96},{96,112},{112,128},... | collective-permute-start | bytes 1179656 | tf_op jit(solution)/shard_map/ppermute | solution.py:14
  61.8 14.9 %collective-permute-start.5 = (bf16[768,256]{1,0:T(8,128)(2,1)S(1)}, bf16[768,256]{1,0:T(8,128)(2,1)S(1)}, u32[]{:S(2)}, u32[]{:S(2)}) collective-permute-start(bf16[768,256]{1,0:T(8,128)(2,1)S(1)} %fusion.7), channel_id=1, source_target_pairs={{16,0},{32,16},{48,32},{64,48},{80,64},{96,80},{112,96},{128,112},... | collective-permute-start | bytes 1179656 | tf_op jit(solution)/shard_map/ppermute | solution.py:15
  82.4 271.1 %reduce-scatter.2.cloned.1.call-start = ((), (), s32[]{:S(2)}) async-start(), calls=%async_computation.2 | async-start | bytes 4325376 | tf_op jit(solution)/shard_map/reduce_scatter | solution.py:55
  180.7 419.6 %copy-start.2 = (bf16[12,256,64]{1,2,0:T(8,128)(2,1)S(1)}, bf16[12,256,64]{1,2,0:T(8,128)(2,1)}, u32[]{:S(2)}) copy-start(bf16[12,256,64]{1,2,0:T(8,128)(2,1)} %fusion.4) | copy-start | bytes 1179652
  180.7 419.6 %all-gather.5.cloned.1.call-start = ((), (), s32[]{:S(2)}) async-start(), calls=%async_computation.3 | async-start | bytes 2162688 | tf_op jit(solution)/shard_map/all_gather | solution.py:63
Sparse Core Ops, SparseCore 0:
  82.5 91.4 all-gather.2
  180.8 172.6 reduce-scatter.1
  450.7 149.4 all-gather.4
where the time goes:
time: 613 us
  waiting for transfers between devices  435 us (71%)
  blocking collectives  93.4 us (15%)
  starting transfers between devices  36.4 us (6%)
  matrix products  20.6 us (3%)
  between operations  14.4 us (2%)
  local copies, waits for them, and re-layouts  7.51 us (1%)
    reduce_scatter x1, waiting for transfers between devices, local(): lax.psum_scatter(partial_gram, 'elem', scatter_dimension=0, tiled=True)  173 us
    all_gather x1, waiting for transfers between devices, local(): scaled = lax.all_gather(scaled_part, 'elem', axis=0, tiled=True)  149 us
    psum x1, blocking collectives, local(): total = lax.psum(own_diagonal, ('elem', 'orb'))  93.4 us
    all_gather x1, waiting for transfers between devices, local(): panel = lax.all_gather(filtered, 'orb', axis=1, tiled=True)  91.5 us
    ppermute x3, starting transfers between devices, extended_2(): after = lax.ppermute(initial, axis, down)  28.1 us
    ppermute x3, waiting for transfers between devices, extended_2(): before = lax.ppermute(last, axis, up)  18.2 us
  transfers between devices with their start and end apart: 9, of which 9 were waited for; matrix products, arithmetic and copies ran while one was open for 0% of the time, Pallas kernels for 0%

commit v1 on v0

--- a/solution.py
+++ b/solution.py
@@ -48,7 +48,9 @@
     groups = lax.axis_size("orb")
     my_group = lax.axis_index("orb")
     orbital_count = columns * groups
-    panel = lax.all_gather(filtered, "orb", axis=1, tiled=True)
+    panel = jnp.concatenate(
+        lax.all_to_all(jnp.stack([filtered] * lax.axis_size("orb")), "orb", 0, 0), axis=1
+    )
     partial_gram = lax.dot_general(
         panel, filtered, (((0,), (0,)), ((), ())), preferred_element_type=jnp.float32
     )

time: 613 us -> 663 us (1.082)
  blocking collectives: 93.4 us -> 236 us
  waiting for transfers between devices: 435 us -> 341 us
    all_to_all x0 -> x1, blocking collectives: none -> 144 us  [local(): lax.all_to_all(jnp.stack([filtered] * lax.axis_size('orb')), 'orb', 0, 0)]
    all_gather x1 -> x0, waiting for transfers between devices: 91.5 us -> none  [local(): panel = lax.all_gather(filtered, 'orb', axis=1, tiled=True)]
  transfers between devices with their start and end apart: 9 -> 8, of which waited for: 9 -> 8; matrix products, arithmetic and copies ran while one was open for 0% -> 0% of each run, Pallas kernels for 0% -> 0%
where the time goes in v1:
time: 663 us; the launch traced here: 662 us
  waiting for transfers between devices  341 us (51%)
  blocking collectives  236 us (36%)
  starting transfers between devices  36.4 us (5%)
  matrix products  17.1 us (3%)
  between operations  14.9 us (2%)
  local copies, waits for them, and re-layouts  10.9 us (2%)
    reduce_scatter x1, waiting for transfers between devices, local(): lax.psum_scatter(partial_gram, 'elem', scatter_dimension=0, tiled=True)  170 us
    all_gather x1, waiting for transfers between devices, local(): scaled = lax.all_gather(scaled_part, 'elem', axis=0, tiled=True)  150 us
    all_to_all x1, blocking collectives, local(): lax.all_to_all(jnp.stack([filtered] * lax.axis_size('orb')), 'orb', 0, 0)  144 us
    psum x1, blocking collectives, local(): total = lax.psum(own_diagonal, ('elem', 'orb'))  92.2 us
    ppermute x3, starting transfers between devices, extended_2(): after = lax.ppermute(initial, axis, down)  28.1 us
    ppermute x3, waiting for transfers between devices, extended_2(): before = lax.ppermute(last, axis, up)  18.2 us
  transfers between devices with their start and end apart: 8, of which 8 were waited for; matrix products, arithmetic and copies ran while one was open for 0% of the time, Pallas kernels for 0%

profile of v1, /device:TPU:2, one launch (start us, length us, event | category | flops | bytes accessed | tf_op | source)
XLA Modules:
  0.0 662.0 jit_solution(8316823797213717524)
XLA Ops:
  6.5 0.0 copy-start
  6.5 0.0 reduce-scatter.2.cloned.1.call-start
  6.5 4.4 collective-permute-start
  10.9 11.6 %collective-permute-start.1 = (bf16[768,256]{1,0:T(8,128)(2,1)}, bf16[768,256]{1,0:T(8,128)(2,1)S(1)}, u32[]{:S(2)}, u32[]{:S(2)}) collective-permute-start(bf16[768,256]{1,0:T(8,128)(2,1)} %param.3), channel_id=1, source_target_pairs={{16,0},{32,16},{48,32},{64,48},{80,64},{96,80},{112,96},{128,112},... | collective-permute-start | bytes 1179656 | tf_op jit(solution)/shard_map/ppermute | solution.py:15
  22.6 0.7 compare_select_fusion
  23.3 0.1 copy.5
  23.4 0.1 reshape.38
  23.5 6.5 collective-permute-done
  30.0 1.3 collective-permute-done.1
  31.3 1.1 pad_maximum_fusion
  32.3 2.4 gather_fusion
  34.8 0.0 copy-done
  34.8 2.4 fusion.13
  37.2 1.9 collective-permute-start.2
  39.1 8.2 %collective-permute-start.3 = (bf16[768,256]{1,0:T(8,128)(2,1)S(1)}, bf16[768,256]{1,0:T(8,128)(2,1)S(1)}, u32[]{:S(2)}, u32[]{:S(2)}) collective-permute-start(bf16[768,256]{1,0:T(8,128)(2,1)S(1)} %bitcast.60), channel_id=1, source_target_pairs={{16,0},{32,16},{48,32},{64,48},{80,64},{96,80},{112,96},{128,112},... | collective-permute-start | bytes 1179656 | tf_op jit(solution)/shard_map/ppermute | solution.py:15
  47.3 6.3 collective-permute-done.2
  53.6 1.2 collective-permute-done.3
  54.8 0.1 pad_maximum_fusion.1
  54.9 2.4 gather_fusion.1
  57.3 0.0 copy-start.2
  57.3 2.4 fusion.2
  59.8 0.0 copy-done.2
  59.8 0.1 fusion.7
  59.9 1.9 collective-permute-start.4
  61.8 8.3 %collective-permute-start.5 = (bf16[768,256]{1,0:T(8,128)(2,1)S(1)}, bf16[768,256]{1,0:T(8,128)(2,1)S(1)}, u32[]{:S(2)}, u32[]{:S(2)}) collective-permute-start(bf16[768,256]{1,0:T(8,128)(2,1)S(1)} %fusion.7), channel_id=1, source_target_pairs={{16,0},{32,16},{48,32},{64,48},{80,64},{96,80},{112,96},{128,112},... | collective-permute-start | bytes 1179656 | tf_op jit(solution)/shard_map/ppermute | solution.py:15
  70.1 5.5 collective-permute-done.4
  75.6 1.2 collective-permute-done.5
  76.7 0.1 pad_maximum_fusion.2
  76.8 2.4 gather_fusion.2
  79.2 2.4 fusion.4
  81.6 0.2 copy.6
  81.8 0.6 stack.2
  82.4 143.9 %all_to_all.5 = bf16[16,768,256]{1,2,0:T(8,128)(2,1)S(1)} all-to-all(bf16[16,768,256]{1,2,0:T(8,128)(2,1)S(1)} %stack.2), channel_id=1, replica_groups=mesh['elem'=32,'orb'=16] {'orb'}, dimensions={0} | all-to-all | bytes 12582912 | tf_op jit(solution)/shard_map/all_to_all | solution.py:52
  226.3 0.0 copy-start.1
  226.3 2.7 copy-done.1
  229.0 3.9 fusion.14
  232.9 0.0 reduce-scatter.2.cloned.1.call-update
  232.9 0.0 all-gather.2.cloned.1.call-start
  233.0 169.6 %reduce-scatter.2.cloned.1.call-done = f32[128,256]{1,0:T(8,128)} async-done(((f32[4096,256]{1,0:T(8,128)}), f32[128,256]{1,0:T(8,128)}) %reduce-scatter.2.cloned.1.call-update) | async-done | bytes 131088 | tf_op jit(solution)/shard_map/reduce_scatter | solution.py:57
  402.5 1.6 select_reduce_fusion
  404.2 92.2 %psum.7 = f32[]{:T(128)} all-reduce(f32[]{:T(128)} %select_reduce_fusion), channel_id=1, replica_groups=mesh['elem'=32,'orb'=16] {'elem','orb'}, use_global_device_ids=true, to_apply=%region_2.3 | all-reduce | flops 1 | bytes 8 | tf_op jit(solution)/shard_map/psum | solution.py:62
  497.1 1.6 divide_convert_fusion
  498.6 0.0 all-gather.2.cloned.1.call-update
  499.3 149.8 %all-gather.2.cloned.1.call-done = bf16[4096,256]{1,0:T(8,128)(2,1)} async-done(((bf16[128,256]{1,0:T(8,128)(2,1)}), bf16[4096,256]{1,0:T(8,128)(2,1)}) %all-gather.2.cloned.1.call-update) | async-done | bytes 2097168 | tf_op jit(solution)/shard_map/all_gather | solution.py:65
  649.1 6.0 fusion.6
  (3 shorter events, 0.0 us)
Async XLA Ops:
  6.5 28.2 %copy-start = (bf16[12,7,64,64]{3,2,1,0:T(8,128)(2,1)S(1)}, bf16[12,7,64,64]{3,2,1,0:T(8,128)(2,1)}, u32[]{:S(2)}) copy-start(bf16[12,7,64,64]{3,2,1,0:T(8,128)(2,1)} %param.4) | copy-start | bytes 2064388
  6.5 396.0 %reduce-scatter.2.cloned.1.call-start = ((), (), s32[]{:S(2)}) async-start(), calls=%async_computation.2 | async-start | bytes 4325376 | tf_op jit(solution)/shard_map/reduce_scatter | solution.py:57
  6.5 23.4 %collective-permute-start = (bf16[768,256]{1,0:T(8,128)(2,1)}, bf16[768,256]{1,0:T(8,128)(2,1)S(1)}, u32[]{:S(2)}, u32[]{:S(2)}) collective-permute-start(bf16[768,256]{1,0:T(8,128)(2,1)} %param.3), channel_id=1, source_target_pairs={{0,16},{16,32},{32,48},{48,64},{64,80},{80,96},{96,112},{112,128},... | collective-permute-start | bytes 1179656 | tf_op jit(solution)/shard_map/ppermute | solution.py:14
  10.9 20.3 %collective-permute-start.1 = (bf16[768,256]{1,0:T(8,128)(2,1)}, bf16[768,256]{1,0:T(8,128)(2,1)S(1)}, u32[]{:S(2)}, u32[]{:S(2)}) collective-permute-start(bf16[768,256]{1,0:T(8,128)(2,1)} %param.3), channel_id=1, source_target_pairs={{16,0},{32,16},{48,32},{64,48},{80,64},{96,80},{112,96},{128,112},... | collective-permute-start | bytes 1179656 | tf_op jit(solution)/shard_map/ppermute | solution.py:15
  37.2 16.4 %collective-permute-start.2 = (bf16[768,256]{1,0:T(8,128)(2,1)S(1)}, bf16[768,256]{1,0:T(8,128)(2,1)S(1)}, u32[]{:S(2)}, u32[]{:S(2)}) collective-permute-start(bf16[768,256]{1,0:T(8,128)(2,1)S(1)} %bitcast.59), channel_id=1, source_target_pairs={{0,16},{16,32},{32,48},{48,64},{64,80},{80,96},{96,112},{112,128},... | collective-permute-start | bytes 1179656 | tf_op jit(solution)/shard_map/ppermute | solution.py:14
  39.1 15.7 %collective-permute-start.3 = (bf16[768,256]{1,0:T(8,128)(2,1)S(1)}, bf16[768,256]{1,0:T(8,128)(2,1)S(1)}, u32[]{:S(2)}, u32[]{:S(2)}) collective-permute-start(bf16[768,256]{1,0:T(8,128)(2,1)S(1)} %bitcast.60), channel_id=1, source_target_pairs={{16,0},{32,16},{48,32},{64,48},{80,64},{96,80},{112,96},{128,112},... | collective-permute-start | bytes 1179656 | tf_op jit(solution)/shard_map/ppermute | solution.py:15
  57.3 2.4 copy-start.2
  59.9 15.7 %collective-permute-start.4 = (bf16[768,256]{1,0:T(8,128)(2,1)S(1)}, bf16[768,256]{1,0:T(8,128)(2,1)S(1)}, u32[]{:S(2)}, u32[]{:S(2)}) collective-permute-start(bf16[768,256]{1,0:T(8,128)(2,1)S(1)} %fusion.7), channel_id=1, source_target_pairs={{0,16},{16,32},{32,48},{48,64},{64,80},{80,96},{96,112},{112,128},... | collective-permute-start | bytes 1179656 | tf_op jit(solution)/shard_map/ppermute | solution.py:14
  61.8 14.9 %collective-permute-start.5 = (bf16[768,256]{1,0:T(8,128)(2,1)S(1)}, bf16[768,256]{1,0:T(8,128)(2,1)S(1)}, u32[]{:S(2)}, u32[]{:S(2)}) collective-permute-start(bf16[768,256]{1,0:T(8,128)(2,1)S(1)} %fusion.7), channel_id=1, source_target_pairs={{16,0},{32,16},{48,32},{64,48},{80,64},{96,80},{112,96},{128,112},... | collective-permute-start | bytes 1179656 | tf_op jit(solution)/shard_map/ppermute | solution.py:15
  226.3 2.7 copy-start.1
  232.9 416.3 %all-gather.2.cloned.1.call-start = ((), (), s32[]{:S(2)}) async-start(), calls=%async_computation.3 | async-start | bytes 2162688 | tf_op jit(solution)/shard_map/all_gather | solution.py:65
Sparse Core Ops, SparseCore 0:
  233.0 169.4 reduce-scatter.1
  498.8 150.3 all-gather.1
